TPU v7x, 32 devices: a whole 2x2x4 slice. The times are simulated.
32 devices in a mesh: zs: 4 (over z), ys: 8 (over y, x, core).
Axes of the slice: x: 2, y: 2, z: 4, core: 2. Of those that a mesh axis runs over, the one named last changes fastest.
Arguments:
- polarization: bfloat16 [2, 6, 256, 128, 512], P(None, None, None, 'ys', 'zs'), may hold values from -6 to 6
- theta_index: int32 [512], replicated, may hold values from 0 to 179
- phi_index: int32 [512], replicated, may hold values from 0 to 359
Outputs:
- mueller: float32 [16, 512], replicated
All inputs are finite; a program needn't handle non-finite values.
Results may differ from a plain program's by a relative error of at most 0.0033.
Values sent between devices are 32-bit elements.
A program may use at most 64 MiB of HBM per device.

v0:
```python
import math

import jax
import jax.numpy as jnp
from jax import lax
from jax.sharding import PartitionSpec as P

NTHETA = 180
NPHI = 360


wave_step = 0.6
pauli_set = (((1, 0), (0, 1)), ((1, 0), (0, -1)), ((0, 1), (1, 0)), ((0, -1j), (1j, 0)))


def angles(theta_index, phi_index):
    polar_angle = math.pi * (theta_index.astype(jnp.float32) + 0.5) / NTHETA
    azimuth = 2.0 * math.pi * phi_index.astype(jnp.float32) / NPHI
    return (polar_angle, azimuth)


def mueller_of(amplitude, polar_angle, azimuth):
    unit_theta = (
        jnp.cos(polar_angle) * jnp.cos(azimuth),
        jnp.cos(polar_angle) * jnp.sin(azimuth),
        -jnp.sin(polar_angle),
    )
    unit_phi = (-jnp.sin(azimuth), jnp.cos(azimuth))
    real_jones = [[None, None], [None, None]]
    imag_jones = [[None, None], [None, None]]
    for s, unit_vec in enumerate((unit_theta, unit_phi)):
        for p in range(2):
            real_sum = 0.0
            imag_sum = 0.0
            for c in range(len(unit_vec)):
                real_sum = real_sum + unit_vec[c] * amplitude[:, 3 * p + c]
                imag_sum = imag_sum + unit_vec[c] * amplitude[:, 6 + 3 * p + c]
            real_jones[s][p] = real_sum
            imag_jones[s][p] = imag_sum
    elements = []
    for i in range(4):
        for j in range(4):
            summed = 0.0
            for a in range(2):
                for b in range(2):
                    for c in range(2):
                        for e in range(2):
                            weight = complex(pauli_set[i][a][b]) * complex(pauli_set[j][c][e])
                            if weight == 0:
                                continue
                            z_real = (
                                real_jones[b][c] * real_jones[a][e]
                                + imag_jones[b][c] * imag_jones[a][e]
                            )
                            z_imag = (
                                imag_jones[b][c] * real_jones[a][e]
                                - real_jones[b][c] * imag_jones[a][e]
                            )
                            summed = summed + weight.real * z_real - weight.imag * z_imag
            elements.append(0.5 * summed)
    return jnp.stack(elements)


def body(polarization, theta_index, phi_index):
    halves, components, cells_x, cells_y, cells_z = polarization.shape
    count_y = lax.axis_size("ys")
    count_z = lax.axis_size("zs")
    total_y = cells_y * count_y
    total_z = cells_z * count_z
    polar_angle, azimuth = angles(theta_index, phi_index)
    unit_x = jnp.sin(polar_angle) * jnp.cos(azimuth)
    unit_y = jnp.sin(polar_angle) * jnp.sin(azimuth)
    unit_z = jnp.cos(polar_angle)
    pos_x = (jnp.arange(cells_x) - cells_x // 2).astype(jnp.float32)
    pos_y = (lax.axis_index("ys") * cells_y + jnp.arange(cells_y) - total_y // 2).astype(
        jnp.float32
    )
    pos_z = (lax.axis_index("zs") * cells_z + jnp.arange(cells_z) - total_z // 2).astype(
        jnp.float32
    )
    flattened = polarization.reshape(halves, components, cells_x, cells_y * cells_z)
    scaling = 1.0 / math.sqrt(cells_x * total_y * total_z)
    directions = theta_index.shape[0]
    block_size = 64

    def one_block(first_row):
        bx = lax.dynamic_slice_in_dim(unit_x, first_row, block_size)
        by = lax.dynamic_slice_in_dim(unit_y, first_row, block_size)
        bz = lax.dynamic_slice_in_dim(unit_z, first_row, block_size)
        phase_x = wave_step * bx[:, None] * pos_x[None, :]
        tables = jnp.stack([jnp.cos(phase_x), jnp.sin(phase_x)]).astype(jnp.bfloat16)
        summed = jnp.einsum(
            "tdx,rcxq->tdrcq", tables, flattened, preferred_element_type=jnp.float32
        )
        real_x = summed[0, :, 0] + summed[1, :, 1]
        imag_x = summed[0, :, 1] - summed[1, :, 0]
        phase_yz = wave_step * (
            by[:, None, None] * pos_y[None, :, None] + bz[:, None, None] * pos_z[None, None, :]
        )
        phase_yz = phase_yz.reshape(block_size, cells_y * cells_z)
        cos_yz = jnp.cos(phase_yz)[:, None, :]
        sin_yz = jnp.sin(phase_yz)[:, None, :]
        real_part = jnp.sum(real_x * cos_yz + imag_x * sin_yz, axis=-1)
        imag_part = jnp.sum(imag_x * cos_yz - real_x * sin_yz, axis=-1)
        return jnp.concatenate([real_part, imag_part], axis=1) * scaling

    def amplitudes(start_row, row_count):
        if row_count % block_size == 0:
            firsts = (start_row + jnp.arange(row_count // block_size) * block_size).astype(
                jnp.int32
            )
            return lax.map(one_block, firsts).reshape(row_count, 12)
        block_count = min(row_count // block_size + 2, directions // block_size)
        cover_start = jnp.clip(
            start_row // block_size * block_size, 0, directions - block_count * block_size
        ).astype(jnp.int32)
        firsts = (cover_start + jnp.arange(block_count) * block_size).astype(jnp.int32)
        covered = lax.map(one_block, firsts).reshape(block_count * block_size, 12)
        return lax.dynamic_slice_in_dim(
            covered, (start_row - cover_start).astype(jnp.int32), row_count
        )

    partial_rows = amplitudes(0, directions)
    complete = lax.psum(partial_rows, ("zs", "ys"))
    return mueller_of(complete, polar_angle, azimuth)


def solution(mesh):
    return jax.shard_map(
        body,
        mesh=mesh,
        in_specs=(P(None, None, None, "ys", "zs"), P(), P()),
        out_specs=P(),
        check_vma=False,
    )
```

profile of v0, /device:TPU:0, one launch (start us, length us, event | category | flops | bytes accessed | tf_op | source)
XLA Modules:
  0.0 174.2 jit_solution(4613660026786079865)
XLA Ops:
  0.0 0.7 fusion.25
  0.8 19.3 %reshape.209 = bf16[2,6,256,2048]{3,2,1,0:T(8,128)(2,1)} reshape(bf16[2,6,256,16,128]{4,3,2,1,0:T(8,128)(2,1)} %param.5) | data formatting | bytes 25165824 | tf_op jit(solution)/shard_map/reshape | solution.py:81
  20.1 110.4 %while.11 = (s32[]{:T(128)}, f32[8,64,12]{1,0,2:T(8,128)S(1)}, s32[8]{0:T(128)S(1)}, f32[512]{0:T(512)S(1)}, bf16[2,6,256,2048]{3,2,1,0:T(8,128)(2,1)}, /*index=...) while((s32[]{:T(128)}, f32[8,64,12]{1,0,2:T(8,128)S(1)}, ...), condition=%wide.region_3.4_spmd.clone, body=%wide.region_0.3_spmd.clone.sunk | while | flops 1618930432 | bytes 42175036 | solution.py:112
  20.1 0.7 dynamic_slice.23
  23.1 1.9 %fusion.36 = (f32[64,16,128]{2,1,0:T(8,128)S(1)}, f32[64,16,128]{2,1,0:T(8,128)S(1)}) fusion(f32[64,128]{1,0:T(8,128)S(1)} %broadcast_multiply_fusion.4, f32[64,16]{1,0:T(8,128)S(1)} %broadcast_multiply_fusion.5), kind=kLoop, calls=%fused_computation.15.clone.1 | loop fusion | flops 262144 | bytes 1085440 | tf_op jit(solution)/shard_map/while/body/eval_jaxpr/cos | solution.py:101
  25.8 6.5 %fusion.38 = f32[2,64,2,6,2048]{4,1,3,2,0:T(8,128)S(1)} fusion(bf16[2,6,256,2048]{3,2,1,0:T(8,128)(2,1)} %get-tuple-element.303, bf16[1,64,256]{2,1,0:T(8,128)(2,1)S(1)} %get-tuple-element.271, bf16[1,64,256]{2,1,0:T(8,128)(2,1)S(1)} %get-tuple-element.272), kind=kOutput, calls=%fused_computation.3.clone.1 | convolution fusion | flops 1610743808 | bytes 25231360 | tf_op jit(solution)/shard_map/while/body/eval_jaxpr/tdx,rcxq->tdrcq/dot_general | solution.py:92
  32.2 1.6 add_reduce_fusion.2
  33.9 0.7 dynamic_slice.23
  36.9 1.9 %fusion.36 = (f32[64,16,128]{2,1,0:T(8,128)S(1)}, f32[64,16,128]{2,1,0:T(8,128)S(1)}) fusion(f32[64,128]{1,0:T(8,128)S(1)} %broadcast_multiply_fusion.4, f32[64,16]{1,0:T(8,128)S(1)} %broadcast_multiply_fusion.5), kind=kLoop, calls=%fused_computation.15.clone.1 | loop fusion | flops 262144 | bytes 1085440 | tf_op jit(solution)/shard_map/while/body/eval_jaxpr/cos | solution.py:101
  39.6 6.5 %fusion.38 = f32[2,64,2,6,2048]{4,1,3,2,0:T(8,128)S(1)} fusion(bf16[2,6,256,2048]{3,2,1,0:T(8,128)(2,1)} %get-tuple-element.303, bf16[1,64,256]{2,1,0:T(8,128)(2,1)S(1)} %get-tuple-element.271, bf16[1,64,256]{2,1,0:T(8,128)(2,1)S(1)} %get-tuple-element.272), kind=kOutput, calls=%fused_computation.3.clone.1 | convolution fusion | flops 1610743808 | bytes 25231360 | tf_op jit(solution)/shard_map/while/body/eval_jaxpr/tdx,rcxq->tdrcq/dot_general | solution.py:92
  46.0 1.6 add_reduce_fusion.2
  47.7 0.7 dynamic_slice.23
  50.7 1.9 %fusion.36 = (f32[64,16,128]{2,1,0:T(8,128)S(1)}, f32[64,16,128]{2,1,0:T(8,128)S(1)}) fusion(f32[64,128]{1,0:T(8,128)S(1)} %broadcast_multiply_fusion.4, f32[64,16]{1,0:T(8,128)S(1)} %broadcast_multiply_fusion.5), kind=kLoop, calls=%fused_computation.15.clone.1 | loop fusion | flops 262144 | bytes 1085440 | tf_op jit(solution)/shard_map/while/body/eval_jaxpr/cos | solution.py:101
  53.4 6.5 %fusion.38 = f32[2,64,2,6,2048]{4,1,3,2,0:T(8,128)S(1)} fusion(bf16[2,6,256,2048]{3,2,1,0:T(8,128)(2,1)} %get-tuple-element.303, bf16[1,64,256]{2,1,0:T(8,128)(2,1)S(1)} %get-tuple-element.271, bf16[1,64,256]{2,1,0:T(8,128)(2,1)S(1)} %get-tuple-element.272), kind=kOutput, calls=%fused_computation.3.clone.1 | convolution fusion | flops 1610743808 | bytes 25231360 | tf_op jit(solution)/shard_map/while/body/eval_jaxpr/tdx,rcxq->tdrcq/dot_general | solution.py:92
  59.8 1.6 add_reduce_fusion.2
  64.5 1.9 %fusion.36 = (f32[64,16,128]{2,1,0:T(8,128)S(1)}, f32[64,16,128]{2,1,0:T(8,128)S(1)}) fusion(f32[64,128]{1,0:T(8,128)S(1)} %broadcast_multiply_fusion.4, f32[64,16]{1,0:T(8,128)S(1)} %broadcast_multiply_fusion.5), kind=kLoop, calls=%fused_computation.15.clone.1 | loop fusion | flops 262144 | bytes 1085440 | tf_op jit(solution)/shard_map/while/body/eval_jaxpr/cos | solution.py:101
  67.2 6.5 %fusion.38 = f32[2,64,2,6,2048]{4,1,3,2,0:T(8,128)S(1)} fusion(bf16[2,6,256,2048]{3,2,1,0:T(8,128)(2,1)} %get-tuple-element.303, bf16[1,64,256]{2,1,0:T(8,128)(2,1)S(1)} %get-tuple-element.271, bf16[1,64,256]{2,1,0:T(8,128)(2,1)S(1)} %get-tuple-element.272), kind=kOutput, calls=%fused_computation.3.clone.1 | convolution fusion | flops 1610743808 | bytes 25231360 | tf_op jit(solution)/shard_map/while/body/eval_jaxpr/tdx,rcxq->tdrcq/dot_general | solution.py:92
  73.6 1.6 add_reduce_fusion.2
  78.3 1.9 %fusion.36 = (f32[64,16,128]{2,1,0:T(8,128)S(1)}, f32[64,16,128]{2,1,0:T(8,128)S(1)}) fusion(f32[64,128]{1,0:T(8,128)S(1)} %broadcast_multiply_fusion.4, f32[64,16]{1,0:T(8,128)S(1)} %broadcast_multiply_fusion.5), kind=kLoop, calls=%fused_computation.15.clone.1 | loop fusion | flops 262144 | bytes 1085440 | tf_op jit(solution)/shard_map/while/body/eval_jaxpr/cos | solution.py:101
  81.0 6.5 %fusion.38 = f32[2,64,2,6,2048]{4,1,3,2,0:T(8,128)S(1)} fusion(bf16[2,6,256,2048]{3,2,1,0:T(8,128)(2,1)} %get-tuple-element.303, bf16[1,64,256]{2,1,0:T(8,128)(2,1)S(1)} %get-tuple-element.271, bf16[1,64,256]{2,1,0:T(8,128)(2,1)S(1)} %get-tuple-element.272), kind=kOutput, calls=%fused_computation.3.clone.1 | convolution fusion | flops 1610743808 | bytes 25231360 | tf_op jit(solution)/shard_map/while/body/eval_jaxpr/tdx,rcxq->tdrcq/dot_general | solution.py:92
  87.4 1.6 add_reduce_fusion.2
  92.1 1.9 %fusion.36 = (f32[64,16,128]{2,1,0:T(8,128)S(1)}, f32[64,16,128]{2,1,0:T(8,128)S(1)}) fusion(f32[64,128]{1,0:T(8,128)S(1)} %broadcast_multiply_fusion.4, f32[64,16]{1,0:T(8,128)S(1)} %broadcast_multiply_fusion.5), kind=kLoop, calls=%fused_computation.15.clone.1 | loop fusion | flops 262144 | bytes 1085440 | tf_op jit(solution)/shard_map/while/body/eval_jaxpr/cos | solution.py:101
  94.8 6.5 %fusion.38 = f32[2,64,2,6,2048]{4,1,3,2,0:T(8,128)S(1)} fusion(bf16[2,6,256,2048]{3,2,1,0:T(8,128)(2,1)} %get-tuple-element.303, bf16[1,64,256]{2,1,0:T(8,128)(2,1)S(1)} %get-tuple-element.271, bf16[1,64,256]{2,1,0:T(8,128)(2,1)S(1)} %get-tuple-element.272), kind=kOutput, calls=%fused_computation.3.clone.1 | convolution fusion | flops 1610743808 | bytes 25231360 | tf_op jit(solution)/shard_map/while/body/eval_jaxpr/tdx,rcxq->tdrcq/dot_general | solution.py:92
  101.2 1.6 add_reduce_fusion.2
  105.9 1.9 %fusion.36 = (f32[64,16,128]{2,1,0:T(8,128)S(1)}, f32[64,16,128]{2,1,0:T(8,128)S(1)}) fusion(f32[64,128]{1,0:T(8,128)S(1)} %broadcast_multiply_fusion.4, f32[64,16]{1,0:T(8,128)S(1)} %broadcast_multiply_fusion.5), kind=kLoop, calls=%fused_computation.15.clone.1 | loop fusion | flops 262144 | bytes 1085440 | tf_op jit(solution)/shard_map/while/body/eval_jaxpr/cos | solution.py:101
  108.6 6.5 %fusion.38 = f32[2,64,2,6,2048]{4,1,3,2,0:T(8,128)S(1)} fusion(bf16[2,6,256,2048]{3,2,1,0:T(8,128)(2,1)} %get-tuple-element.303, bf16[1,64,256]{2,1,0:T(8,128)(2,1)S(1)} %get-tuple-element.271, bf16[1,64,256]{2,1,0:T(8,128)(2,1)S(1)} %get-tuple-element.272), kind=kOutput, calls=%fused_computation.3.clone.1 | convolution fusion | flops 1610743808 | bytes 25231360 | tf_op jit(solution)/shard_map/while/body/eval_jaxpr/tdx,rcxq->tdrcq/dot_general | solution.py:92
  115.0 1.6 add_reduce_fusion.2
  119.7 1.9 %fusion.36 = (f32[64,16,128]{2,1,0:T(8,128)S(1)}, f32[64,16,128]{2,1,0:T(8,128)S(1)}) fusion(f32[64,128]{1,0:T(8,128)S(1)} %broadcast_multiply_fusion.4, f32[64,16]{1,0:T(8,128)S(1)} %broadcast_multiply_fusion.5), kind=kLoop, calls=%fused_computation.15.clone.1 | loop fusion | flops 262144 | bytes 1085440 | tf_op jit(solution)/shard_map/while/body/eval_jaxpr/cos | solution.py:101
  122.4 6.5 %fusion.38 = f32[2,64,2,6,2048]{4,1,3,2,0:T(8,128)S(1)} fusion(bf16[2,6,256,2048]{3,2,1,0:T(8,128)(2,1)} %get-tuple-element.303, bf16[1,64,256]{2,1,0:T(8,128)(2,1)S(1)} %get-tuple-element.271, bf16[1,64,256]{2,1,0:T(8,128)(2,1)S(1)} %get-tuple-element.272), kind=kOutput, calls=%fused_computation.3.clone.1 | convolution fusion | flops 1610743808 | bytes 25231360 | tf_op jit(solution)/shard_map/while/body/eval_jaxpr/tdx,rcxq->tdrcq/dot_general | solution.py:92
  128.8 1.6 add_reduce_fusion.2
  130.6 42.1 %psum.7 = f32[512,12]{0,1:T(8,128)S(1)} all-reduce(f32[512,12]{0,1:T(8,128)S(1)} %reshape.210), channel_id=1, replica_groups=mesh['zs'=4,'ys'=8] {'zs','ys'}, use_global_device_ids=true, to_apply=%region_4.5 | all-reduce | flops 6144 | bytes 49152 | tf_op jit(solution)/shard_map/psum | solution.py:124
  172.9 1.3 stack.73
  (123 shorter events, 12.4 us)
Async XLA Ops:
  20.1 152.6 %copy-start = (s32[512]{0:T(512)S(1)}, s32[512]{0:T(512)}, u32[]{:S(2)}) copy-start(s32[512]{0:T(512)} %param.7) | copy-start | bytes 6148
  20.1 152.6 %copy-start.1 = (s32[512]{0:T(512)S(1)}, s32[512]{0:T(512)}, u32[]{:S(2)}) copy-start(s32[512]{0:T(512)} %param.6) | copy-start | bytes 6148
where the time goes:
time: 175 us; the launch traced here: 174 us
  matrix products  51.6 us (29%)
  blocking collectives  42.1 us (24%)
  other arithmetic  33.2 us (19%)
  local copies, waits for them, and re-layouts  30.3 us (17%)
  loops' own time  16.9 us (10%)
    dot_general x8, matrix products, one_block(): jnp.einsum('tdx,rcxq->tdrcq', tables, flattened, preferred_element_type=j...  51.6 us
    psum x1, blocking collectives, body(): complete = lax.psum(partial_rows, ('zs', 'ys'))  42.1 us
    reshape x1, local copies, waits for them, and re-layouts, body(): polarization.reshape(halves, components, cells_x, cells_y * cells_z)  19.3 us
    another operation x1, loops' own time, amplitudes(): return lax.map(one_block, firsts).reshape(row_count, 12)  16.9 us
    cos x8, other arithmetic, one_block(): cos_yz = jnp.cos(phase_yz)[:, None, :]  15.3 us
    reduce_sum x8, other arithmetic, one_block(): real_part = jnp.sum(real_x * cos_yz + imag_x * sin_yz, axis=-1)  12.5 us
    dynamic_slice x8, local copies, waits for them, and re-layouts, amplitudes(): return lax.map(one_block, firsts).reshape(row_count, 12)  5.24 us

commit v1 on v0

v1 whole, which is shorter than its diff:
```python
import functools
import math

import jax
import jax.numpy as jnp
from jax import lax
from jax.experimental import pallas as pl
from jax.experimental.pallas import tpu as pltpu
from jax.sharding import PartitionSpec as P

NTHETA = 180
NPHI = 360
MESH = pl.DeviceIdType.MESH

wave_step = 0.6
pauli_set = (((1, 0), (0, 1)), ((1, 0), (0, -1)), ((0, 1), (1, 0)), ((0, -1j), (1j, 0)))


def angles(theta_index, phi_index):
    polar_angle = math.pi * (theta_index.astype(jnp.float32) + 0.5) / NTHETA
    azimuth = 2.0 * math.pi * phi_index.astype(jnp.float32) / NPHI
    return (polar_angle, azimuth)


def mueller_rows(real_jones, imag_jones):
    rows = []
    for i in range(4):
        for j in range(4):
            summed = 0.0
            for a in range(2):
                for b in range(2):
                    for c in range(2):
                        for e in range(2):
                            weight = complex(pauli_set[i][a][b]) * complex(pauli_set[j][c][e])
                            if weight == 0:
                                continue
                            if weight.real != 0:
                                z_real = (
                                    real_jones[b][c] * real_jones[a][e]
                                    + imag_jones[b][c] * imag_jones[a][e]
                                )
                                summed = summed + weight.real * z_real
                            else:
                                z_imag = (
                                    imag_jones[b][c] * real_jones[a][e]
                                    - real_jones[b][c] * imag_jones[a][e]
                                )
                                summed = summed - weight.imag * z_imag
            rows.append(0.5 * summed)
    return rows


def transform_kernel(pol, cos_x, sin_x, cos_y, sin_y, cos_a, sin_a, out, table, data):
    cells_x, cells_y, cells_z = pol.shape[2:]
    depth = cells_x * cells_y
    width = cos_y.shape[1]
    block = 2 * width

    @pl.when(pl.program_id(0) == 0)
    def build():
        cy = jnp.concatenate([cos_y[...]] * 2, axis=1)
        sy = jnp.concatenate([sin_y[...]] * 2, axis=1)
        for first in range(0, depth, block):
            row = lax.broadcasted_iota(jnp.int32, (cells_x, block), 0)
            column = lax.broadcasted_iota(jnp.int32, (cells_x, block), 1)
            low = (row - first // cells_y) * cells_y
            spread = jnp.where((column >= low) & (column < low + cells_y), 1.0, 0.0).astype(
                jnp.bfloat16
            )
            cx = jnp.dot(cos_x[...], spread, preferred_element_type=jnp.float32)
            sx = jnp.dot(sin_x[...], spread, preferred_element_type=jnp.float32)
            table[:, first : first + block] = (cx * cy - sx * sy).astype(jnp.bfloat16)
            table[:, depth + first : depth + first + block] = (sx * cy + cx * sy).astype(
                jnp.bfloat16
            )

    real = pol[0, 0].reshape(depth, cells_z)
    imag = pol[1, 0].reshape(depth, cells_z)
    data[:depth, :cells_z] = real
    data[depth:, :cells_z] = imag
    data[:depth, cells_z:] = imag
    data[depth:, cells_z:] = -real
    summed = jnp.dot(table[...], data[...], preferred_element_type=jnp.float32)
    g_real = summed[:, :cells_z]
    g_imag = summed[:, cells_z:]
    ca = cos_a[...]
    sa = sin_a[...]
    f_real = g_real * ca + g_imag * sa
    f_imag = g_imag * ca - g_real * sa
    out[0, 0:1, :] = jnp.sum(f_real.T, axis=0, keepdims=True)
    out[0, 1:2, :] = jnp.sum(f_imag.T, axis=0, keepdims=True)


def reduce_kernel(axes, counts, scaling, amp, unit, out, first_buf, second_buf, *sems):
    place = {name: lax.axis_index(name) for name in axes}

    def other(name, step):
        ids = dict(place)
        ids[name] = lax.rem(place[name] + step, counts[name])
        return tuple(ids[n] for n in axes)

    barrier = pltpu.get_barrier_semaphore()
    total = 0
    for name in axes:
        for step in range(1, counts[name]):
            pl.semaphore_signal(barrier, inc=1, device_id=other(name, step), device_id_type=MESH)
            total += 1

    rows = []
    for half in range(2):
        for s in range(2):
            for p in range(2):
                summed = 0.0
                for c in range(3 - s):
                    summed = summed + unit[3 * s + c : 3 * s + c + 1, :] * amp[
                        3 * p + c, half : half + 1, :
                    ]
                rows.append(summed * scaling)
    local = jnp.concatenate(rows, axis=0)
    pl.semaphore_wait(barrier, total)

    for stage, (name, buf) in enumerate(zip(reversed(axes), (first_buf, second_buf))):
        send, recv = sems[2 * stage], sems[2 * stage + 1]
        me = place[name]
        buf[me] = local
        copies = []
        for step in range(1, counts[name]):
            copy = pltpu.make_async_remote_copy(
                src_ref=buf.at[me],
                dst_ref=buf.at[me],
                send_sem=send.at[step],
                recv_sem=recv.at[step],
                device_id=other(name, step),
                device_id_type=MESH,
            )
            copy.start()
            copies.append(copy)
        for copy in copies:
            copy.wait()
        local = buf[0]
        for slot in range(1, counts[name]):
            local = local + buf[slot]

    def entry(half, s, p):
        at = 4 * half + 2 * s + p
        return local[at : at + 1, :]

    real_jones = [[entry(0, s, p) for p in range(2)] for s in range(2)]
    imag_jones = [[entry(1, s, p) for p in range(2)] for s in range(2)]
    for at, row in enumerate(mueller_rows(real_jones, imag_jones)):
        out[at : at + 1, :] = row


def body(axes, counts, polarization, theta_index, phi_index):
    halves, components, cells_x, cells_y, cells_z = polarization.shape
    total_y = cells_y * counts["ys"]
    total_z = cells_z * counts["zs"]
    directions = theta_index.shape[0]
    polar_angle, azimuth = angles(theta_index, phi_index)
    sin_t, cos_t = jnp.sin(polar_angle), jnp.cos(polar_angle)
    sin_p, cos_p = jnp.sin(azimuth), jnp.cos(azimuth)
    unit_x = sin_t * cos_p
    unit_y = sin_t * sin_p
    unit_z = cos_t
    scaling = 1.0 / math.sqrt(cells_x * total_y * total_z)

    pos_x = (jnp.arange(cells_x) - cells_x // 2).astype(jnp.float32)
    phase_x = wave_step * unit_x[:, None] * pos_x[None, :]
    cos_x = jnp.cos(phase_x).astype(jnp.bfloat16)
    sin_x = jnp.sin(phase_x).astype(jnp.bfloat16)

    lanes = 128
    centre_y = 0.5 * (cells_y - 1)
    pos_y = (jnp.arange(lanes) % cells_y).astype(jnp.float32) - centre_y
    phase_y = wave_step * unit_y[:, None] * pos_y[None, :]
    offset_y = (lax.axis_index("ys") * cells_y - total_y // 2).astype(jnp.float32) + centre_y
    pos_z = (lax.axis_index("zs") * cells_z + jnp.arange(cells_z) - total_z // 2).astype(
        jnp.float32
    )
    phase_a = wave_step * (unit_y[:, None] * offset_y + unit_z[:, None] * pos_z[None, :])
    depth = cells_x * cells_y

    def whole(array):
        return pl.BlockSpec(array.shape, lambda c: (0, 0))

    small = (cos_x, sin_x, jnp.cos(phase_y), jnp.sin(phase_y), jnp.cos(phase_a), jnp.sin(phase_a))
    amp = pl.pallas_call(
        transform_kernel,
        grid=(components,),
        out_shape=jax.ShapeDtypeStruct((components, 8, directions), jnp.float32),
        in_specs=[
            pl.BlockSpec((halves, 1, cells_x, cells_y, cells_z), lambda c: (0, c, 0, 0, 0))
        ]
        + [whole(array) for array in small],
        out_specs=pl.BlockSpec((1, 8, directions), lambda c: (c, 0, 0)),
        scratch_shapes=[
            pltpu.VMEM((directions, 2 * depth), jnp.bfloat16),
            pltpu.VMEM((2 * depth, 2 * cells_z), jnp.bfloat16),
        ],
        compiler_params=pltpu.CompilerParams(dimension_semantics=("arbitrary",)),
    )(polarization, *small)

    zero = jnp.zeros_like(sin_t)
    unit = jnp.stack([cos_t * cos_p, cos_t * sin_p, -sin_t, -sin_p, cos_p, zero, zero, zero])
    first, second = reversed(axes)
    return pl.pallas_call(
        functools.partial(reduce_kernel, axes, counts, scaling),
        out_shape=jax.ShapeDtypeStruct((16, directions), jnp.float32),
        in_specs=[pl.BlockSpec(memory_space=pltpu.VMEM)] * 2,
        out_specs=pl.BlockSpec(memory_space=pltpu.VMEM),
        scratch_shapes=[
            pltpu.VMEM((counts[first], 8, directions), jnp.float32),
            pltpu.VMEM((counts[second], 8, directions), jnp.float32),
            pltpu.SemaphoreType.DMA((counts[first],)),
            pltpu.SemaphoreType.DMA((counts[first],)),
            pltpu.SemaphoreType.DMA((counts[second],)),
            pltpu.SemaphoreType.DMA((counts[second],)),
        ],
        compiler_params=pltpu.CompilerParams(collective_id=0, has_side_effects=True),
    )(amp, unit)


def solution(mesh):
    axes = tuple(mesh.axis_names)
    counts = dict(mesh.shape)
    return jax.shard_map(
        functools.partial(body, axes, counts),
        mesh=mesh,
        in_specs=(P(None, None, None, "ys", "zs"), P(), P()),
        out_specs=P(),
        check_vma=False,
    )
```

time: 175 us -> 45 us (0.26)
  matrix products: 51.6 us -> 0 us
  blocking collectives: 42.1 us -> 0 us
  Pallas kernels: 0 us -> 35.8 us
  local copies, waits for them, and re-layouts: 30.3 us -> 2.01 us
  other arithmetic: 33.2 us -> 6.96 us
  loops' own time: 16.9 us -> 0 us
    dot_general x8 -> x0, matrix products: 51.6 us -> none  [one_block(): jnp.einsum('tdx,rcxq->tdrcq', tables, flattened, preferred_element_type=j...]
    psum x1 -> x0, blocking collectives: 42.1 us -> none  [body(): complete = lax.psum(partial_rows, ('zs', 'ys'))]
    pallas_call x0 -> x2, Pallas kernels: none -> 35.8 us  [the longest x1 22 us: body(): pl.pallas_call(transform_kernel, grid=(components,), out_shape=jax.ShapeD...]
    reshape x2 -> x0, local copies, waits for them, and re-layouts: 19.4 us -> none  [the longest x1 19.3 us: body(): polarization.reshape(halves, components, cells_x, cells_y * cells_z)]
    another operation x1 -> x0, loops' own time: 16.9 us -> none  [amplitudes(): return lax.map(one_block, firsts).reshape(row_count, 12)]
    cos x8 -> x0, other arithmetic: 15.3 us -> none  [one_block(): cos_yz = jnp.cos(phase_yz)[:, None, :]]
    reduce_sum x8 -> x0, other arithmetic: 12.5 us -> none  [one_block(): real_part = jnp.sum(real_x * cos_yz + imag_x * sin_yz, axis=-1)]
    dynamic_slice x24 -> x0, local copies, waits for them, and re-layouts: 6.44 us -> none  [the longest x8 5.24 us: amplitudes(): return lax.map(one_block, firsts).reshape(row_count, 12)]
where the time goes in v1:
time: 45 us; the launch traced here: 44.8 us
  Pallas kernels  35.8 us (80%)
  other arithmetic  6.96 us (15%)
  local copies, waits for them, and re-layouts  2.01 us (4%)
    pallas_call x1, Pallas kernels, body(): pl.pallas_call(transform_kernel, grid=(components,), out_shape=jax.ShapeD...  22 us
    pallas_call x1, Pallas kernels, body(): pl.pallas_call(functools.partial(reduce_kernel, axes, counts, scaling), o...  13.8 us
    sin x1, other arithmetic, body(): jnp.sin(phase_y)  3.2 us
    convert_element_type x1, other arithmetic, body(): sin_x = jnp.sin(phase_x).astype(jnp.bfloat16)  2.99 us
    unnamed x1, local copies, waits for them, and re-layouts  1.38 us

profile of v1, /device:TPU:0, one launch (start us, length us, event | category | flops | bytes accessed | tf_op | source)
XLA Modules:
  0.0 44.8 jit_solution(6739573190648212372)
XLA Ops:
  0.0 0.8 %fusion.9 = (f32[512]{0:T(512)S(1)}, f32[512]{0:T(512)S(1)}, f32[512]{0:T(512)S(1)}, f32[512]{0:T(512)S(1)}, f32[512]{0:T(512)S(1)}, /*index=5*/f32[512]{0:T(512...) fusion(s32[512]{0:T(512)} %param.5, s32[512]{0:T(512)} %param.4, f32[]{:T(128)S(6)} %add.56), kind=kLoop, calls=%fused_computation.18 | loop fusion | flops 7168 | bytes 22532 | tf_op jit(solution)/shard_map/mul | solution.py:204
  0.8 3.2 %multiply_sine_fusion.1 = (f32[512,128]{1,0:T(8,128)}, f32[512,128]{1,0:T(8,128)}, f32[512,128]{1,0:T(8,128)}, f32[512,128]{1,0:T(8,128)}) fusion(f32[128]{0:T(128)S(1)} %fusion.13, f32[512]{0:T(512)S(1)} %get-tuple-element.11, f32[128]{0:T(128)S(1)} %add_convert_fusion.1, f32[512]{0:T(512)S(1)} %get-tuple-element.18, f32[512]{0:T(512)S(1)} %get-tuple-element.10), kind=kLoop, calls=%fused_computation.4 | loop fusion | flops 262144 | bytes 1055744 | tf_op jit(solution)/shard_map/sin | solution.py:186
  4.0 3.0 %fusion.1 = (bf16[512,256]{1,0:T(8,128)(2,1)}, bf16[512,256]{1,0:T(8,128)(2,1)}) fusion(f32[256]{0:T(256)S(1)} %add_convert_fusion, f32[512]{0:T(512)S(1)} %get-tuple-element.8), kind=kLoop, calls=%fused_computation.3 | loop fusion | flops 393216 | bytes 527360 | tf_op jit(solution)/shard_map/convert_element_type | solution.py:170
  7.0 22.0 %shard_map.37.amp = f32[6,8,512]{2,1,0:T(8,128)} custom-call(bf16[2,6,256,16,128]{4,3,2,1,0:T(8,128)(2,1)} %pol.1, bf16[512,256]{1,0:T(8,128)(2,1)} %get-tuple-element.13.cos_x, bf16[512,256]{1,0:T(8,128)(2,1)} %get-tuple-element.12.sin_x, f32[512,128]{1,0:T(8,128)} %get-tuple-element.15.cos_y, f32[512,128]{1,0:T(8,128)} %get-tuple-element.14.sin_y, ...), custom_call_target="tpu_custom_call" | custom-call | tf_op jit(solution)/shard_map/pallas_call | solution.py:187
  29.0 0.6 %stack.27.unit = f32[8,512]{1,0:T(8,128)} concatenate(f32[1,512]{1,0:T(1,128)S(1)} %bitcast.6, f32[1,512]{1,0:T(1,128)S(1)} %bitcast.5, f32[1,512]{1,0:T(1,128)S(1)} %bitcast.8, f32[1,512]{1,0:T(1,128)S(1)} %bitcast.9, f32[1,512]{1,0:T(1,128)S(1)} %bitcast.7, f32[1,512]{1,0:T(1,128)S(1)} %stack_broadcast_in_dim.3, f32[2,512]{1,0:T(2,128)S(1)} %stack.26), dimensions={0} | concatenate | bytes 32768 | tf_op jit(solution)/shard_map/stack | solution.py:204
  29.6 13.8 %shard_map.38 = f32[16,512]{1,0:T(8,128)} custom-call(f32[6,8,512]{2,1,0:T(8,128)} %shard_map.37.amp, f32[8,512]{1,0:T(8,128)} %stack.27.unit), custom_call_target="tpu_custom_call" | custom-call | tf_op jit(solution)/shard_map/pallas_call | solution.py:206
  43.4 1.4 %copy.5 = f32[16,512]{1,0:T(8,128)} copy(f32[16,512]{1,0:T(8,128)} %shard_map.38) | data formatting | bytes 65536
  (5 shorter events, 0.0 us)
